TPU v7x, 512 devices: a whole 4x8x8 slice. The times are simulated.
512 devices in a mesh: tile: 64 (over z, x, core), tm: 8 (over y).
Axes of the slice: x: 4, y: 8, z: 8, core: 2. Of those that a mesh axis runs over, the one named last changes fastest.
Arguments:
- data: bfloat16 [8192, 64, 128], P('tile', 'tm'), may hold values from -8 to 8
- send_list: int32 [64, 64, 8], P('tile'), may hold values from 0 to 127
- footprint_slot: int32 [8192, 8], P('tile'), may hold values from 0 to 511, as said below
- footprint: bfloat16 [8192, 8, 128], P('tile'), may hold values from 0 to 0.053955078
- colour: int32 [8192], P('tile'), may hold values from 0 to 3, as said below
- correlation: int32 [8192, 8], P('tile'), may hold values from 0 to 8191, as said below
- correlation_gram: float32 [8192, 8], P('tile'), may hold values from 0.01 to 0.15
- traces_init: float32 [64, 8192], P('tm', 'tile'), may hold values from 0 to 4
Outputs:
- traces: float32 [64, 8192], P('tm', 'tile')
- trace_rms: float32 [8192], P('tile')
Inputs may be any that keep to these rules, and one draw needn't show every extreme that they name: footprint_slot[k, j] names the slot c = footprint_slot[k, j] % 8 in which tile device footprint_slot[k, j] // 8 sends a block to the owner of k, tile device k // 128; the 8 slots of one footprint differ. Each tile device owns exactly a quarter of its 128 components in each colour; every listed neighbour has a colour other than the component's own. `correlation`: the tile axis folds the slab's two halves end to end, so the neighbours of a component owned by tile device d are owned by tile device d - 1, d, d + 1 or (d + 32) modulo 64; entries may repeat.
All inputs are finite; a program needn't handle non-finite values.
Results may differ from a plain program's by a relative error of at most 0.0003.
Values may be sent and summed in bfloat16 or wider, within the bound.
A program may use at most 64 MiB of HBM per device.

v0:
```python
import jax
import jax.numpy as jnp
from jax import lax
from jax.sharding import PartitionSpec as P


def shards(
    data, send_list, footprint_slot, footprint, colour, correlation, correlation_gram, traces_init
):
    tile_count = lax.axis_size("tile")
    tile_here = lax.axis_index("tile")
    comp_count = colour.shape[0]
    quarter = comp_count // 4
    frames_dev = data.shape[1]
    voxels = data.shape[2]
    cap_slots = send_list.shape[2]
    slot_count = tile_count * cap_slots
    blocks_fp = footprint.shape[1]
    listed = correlation.shape[1]
    outgoing = data[send_list[0].reshape(-1)].reshape(tile_count, cap_slots, frames_dev, voxels)
    arrived = lax.all_to_all(outgoing, "tile", split_axis=0, concat_axis=0, tiled=True).reshape(
        slot_count, frames_dev, voxels
    )
    weights32 = footprint.astype(jnp.float32)
    self_gram = jnp.sum(weights32 * weights32, axis=(1, 2))
    comp_block = min(32, comp_count)
    block_total = comp_count // comp_block
    slot_range = jnp.arange(slot_count, dtype=jnp.int32)

    def project(inputs):
        slot_ids, weight_rows = inputs
        one_hot = (slot_ids[:, :, None] == slot_range[None, None, :]).astype(jnp.bfloat16)
        spread = jnp.einsum(
            "kjs,kjv->svk", one_hot, weight_rows, preferred_element_type=jnp.bfloat16
        )
        return jnp.einsum("sfv,svk->fk", arrived, spread, preferred_element_type=jnp.float32)

    pieces = lax.map(
        project,
        (
            footprint_slot.reshape(block_total, comp_block, blocks_fp),
            footprint.reshape(block_total, comp_block, blocks_fp, voxels),
        ),
    )
    projected = jnp.transpose(pieces, (1, 0, 2)).reshape(frames_dev, comp_count)
    ordering = jnp.argsort(colour, stable=True)
    grouped = jnp.argsort(ordering)
    rank_in = grouped % quarter
    proj_group = projected[:, ordering].reshape(frames_dev, 4, quarter)
    gram_group = self_gram[ordering].reshape(4, quarter)
    nb_group = correlation[ordering].reshape(4, quarter, listed)
    weight_group = correlation_gram[ordering].reshape(4, quarter, listed)
    start_group = traces_init[:, ordering].reshape(frames_dev, 4, quarter)
    own_flat = colour * (tile_count * quarter) + tile_here * quarter + rank_in
    table, flat_all = (
        lax.all_gather(start_group, "tile", axis=2, tiled=True),
        lax.all_gather(own_flat, "tile", axis=0, tiled=True),
    )
    span_width = tile_count * quarter
    lookup = flat_all[nb_group]
    fresh_parts = []
    for step_colour in range(4):
        flat_table = table.reshape(frames_dev, 4 * span_width)
        values = jnp.take(flat_table, lookup[step_colour].reshape(-1), axis=1).reshape(
            frames_dev, quarter, listed
        )
        neighbour_sum = jnp.sum(values * weight_group[step_colour][None, :, :], axis=2)
        fresh = jnp.maximum(
            (proj_group[:, step_colour, :] - neighbour_sum) / gram_group[step_colour][None, :], 0.0
        )
        fresh_parts.append(fresh)
        if step_colour + 1 < 4:
            arrived_colour = lax.all_gather(fresh, "tile", axis=1, tiled=True)
            table = table.at[:, step_colour, :].set(arrived_colour)
    final_group = jnp.stack(fresh_parts, axis=1).reshape(frames_dev, comp_count)
    traces = final_group[:, grouped]
    energy_sum = lax.psum(jnp.sum(traces * traces, axis=0), "tm")
    trace_rms = jnp.sqrt(energy_sum / (frames_dev * lax.axis_size("tm")) + 1e-06)
    return (traces, trace_rms)


def solution(mesh):
    placed = (
        P("tile", "tm", None),
        P("tile", None, None),
        P("tile", None),
        P("tile", None, None),
        P("tile"),
        P("tile", None),
        P("tile", None),
        P("tm", "tile"),
    )
    return jax.shard_map(
        shards, mesh=mesh, in_specs=placed, out_specs=(P("tm", "tile"), P("tile")), check_vma=False
    )
```

profile of v0, /device:TPU:1, one launch (start us, length us, event | category | flops | bytes accessed | tf_op | source)
XLA Modules:
  0.0 361.1 jit_solution(10333032754767358957)
XLA Ops:
  1.6 2.4 gather_fusion
  4.0 14.8 %all-to-all-start = ((bf16[64,8,8,128]{3,2,1,0:T(8,128)(2,1)}), bf16[64,8,8,128]{3,2,1,0:T(8,128)(2,1)S(1)}, u32[]{:S(2)}, u32[]{:S(2)}) async-start(bf16[64,8,8,128]{3,2,1,0:T(8,128)(2,1)} %bitcast.2), calls=%async_computation | async-start | bytes 2097152 | tf_op jit(solution)/shard_map/all_to_all | solution.py:21
  19.9 2.5 sort.34
  22.5 2.5 sort.35
  25.2 1.2 gather_fusion.6
  28.7 49.7 %all-gather = s32[64,1,128]{2,1,0:T(1,128)S(1)} all-gather(s32[1,1,128]{2,1,0:T(1,128)S(1)} %get-tuple-element.152), channel_id=1, replica_groups=mesh['tile'=64,'tm'=8] {'tile'}, dimensions={0}, use_global_device_ids=true | all-gather | bytes 33280 | tf_op jit(solution)/shard_map/all_gather | solution.py:57
  78.4 6.1 %gather_fusion.4 = s32[1024]{0:T(1024)S(1)} fusion(s32[8192]{0:T(1024)S(1)} %bitcast.154, s32[1024]{0:T(1024)S(1)} %broadcast_clamp_fusion), kind=kCustom, calls=%fused_computation.8 | custom fusion | bytes 12288 | tf_op jit(solution)/shard_map/gather | solution.py:60
  84.6 54.6 %all_gather.15 = f32[8,4,2048]{0,2,1:T(8,128)} all-gather(f32[8,4,32]{0,2,1:T(8,128)S(1)} %bitcast.173), channel_id=1, replica_groups=mesh['tile'=64,'tm'=8] {'tile'}, dimensions={2}, use_global_device_ids=true | all-gather | bytes 266240 | tf_op jit(solution)/shard_map/all_gather | solution.py:56
  139.2 2.9 gather_fusion.8
  142.4 59.1 %while.14 = (s32[]{:T(128)}, f32[4,8,32]{2,1,0:T(8,128)S(1)}, bf16[4,32,8,128]{3,2,1,0:T(8,128)(2,1)S(1)}, s32[4,32,8]{1,0,2:T(4,128)S(1)}, bf16[512,8,128]{2,1,0:T(8,128)(2,1)S(1)}, /*index=5*/s32[]{:T(128)}) while((s32[]{:T(128)}, f32[4,8,32]{2,1,0:T(8,128)S(1)}, bf16[4,32,8,128]{3,2,1,0:T(8,128)(2,1)S(1)}, ...), condition=%wide.region_1.2_spmd.clone, body=%wide.region_0.0_spmd.clone.sunk | while | flops 67239936 | bytes 17915992 | solution.py:38
  142.5 3.3 convolution_bitcast_fusion.3
  145.8 8.0 %copy.102 = bf16[512,128,32]{1,2,0:T(8,128)(2,1)} copy(bf16[512,128,32]{0,1,2:T(8,128)(2,1)} %convolution_bitcast_fusion.3) | data formatting | bytes 8388608 | tf_op jit(solution)/shard_map/while/body/eval_jaxpr/kjs,kjv->svk/transpose | solution.py:33
  153.8 3.4 fusion.42
  157.3 3.3 convolution_bitcast_fusion.3
  160.5 8.0 %copy.102 = bf16[512,128,32]{1,2,0:T(8,128)(2,1)} copy(bf16[512,128,32]{0,1,2:T(8,128)(2,1)} %convolution_bitcast_fusion.3) | data formatting | bytes 8388608 | tf_op jit(solution)/shard_map/while/body/eval_jaxpr/kjs,kjv->svk/transpose | solution.py:33
  168.6 3.4 fusion.42
  172.0 3.3 convolution_bitcast_fusion.3
  175.3 8.0 %copy.102 = bf16[512,128,32]{1,2,0:T(8,128)(2,1)} copy(bf16[512,128,32]{0,1,2:T(8,128)(2,1)} %convolution_bitcast_fusion.3) | data formatting | bytes 8388608 | tf_op jit(solution)/shard_map/while/body/eval_jaxpr/kjs,kjv->svk/transpose | solution.py:33
  183.4 3.4 fusion.42
  186.8 3.3 convolution_bitcast_fusion.3
  190.1 8.0 %copy.102 = bf16[512,128,32]{1,2,0:T(8,128)(2,1)} copy(bf16[512,128,32]{0,1,2:T(8,128)(2,1)} %convolution_bitcast_fusion.3) | data formatting | bytes 8388608 | tf_op jit(solution)/shard_map/while/body/eval_jaxpr/kjs,kjv->svk/transpose | solution.py:33
  198.1 3.4 fusion.42
  202.4 43.2 %all-gather.1 = f32[64,32,8]{1,2,0:T(8,128)S(1)} all-gather(f32[1,32,8]{1,2,0:T(8,128)S(1)} %copy.88), channel_id=1, replica_groups=mesh['tile'=64,'tm'=8] {'tile'}, dimensions={0}, use_global_device_ids=true | all-gather | bytes 66560 | tf_op jit(solution)/shard_map/all_gather | solution.py:73
  246.1 1.1 constant_dynamic-update-slice_fusion.2
  247.2 2.9 gather_fusion.9
  250.4 42.1 %all-gather.2 = f32[64,32,8]{1,2,0:T(8,128)S(1)} all-gather(f32[1,32,8]{1,2,0:T(8,128)S(1)} %copy.91), channel_id=1, replica_groups=mesh['tile'=64,'tm'=8] {'tile'}, dimensions={0}, use_global_device_ids=true | all-gather | bytes 66560 | tf_op jit(solution)/shard_map/all_gather | solution.py:73
  293.0 1.1 constant_dynamic-update-slice_fusion.1
  294.2 2.9 gather_fusion.10
  297.4 43.1 %all-gather.3 = f32[64,32,8]{1,2,0:T(8,128)S(1)} all-gather(f32[1,32,8]{1,2,0:T(8,128)S(1)} %copy.94), channel_id=1, replica_groups=mesh['tile'=64,'tm'=8] {'tile'}, dimensions={0}, use_global_device_ids=true | all-gather | bytes 66560 | tf_op jit(solution)/shard_map/all_gather | solution.py:73
  341.0 1.1 constant_dynamic-update-slice_fusion
  342.0 2.9 gather_fusion.11
  345.9 13.9 %psum.7 = f32[128]{0:T(128)S(1)} all-reduce(f32[128]{0:T(128)S(1)} %multiply_reduce_fusion.1), channel_id=1, replica_groups=mesh['tile'=64,'tm'=8] {'tm'}, use_global_device_ids=true, to_apply=%region_10.12 | all-reduce | flops 128 | bytes 1024 | tf_op jit(solution)/shard_map/psum | solution.py:77
  (79 shorter events, 10.3 us)
Async XLA Ops:
  0.6 1.0 copy-start
  0.6 18.2 %copy-start.1 = (bf16[128,8,128]{2,1,0:T(8,128)(2,1)S(1)}, bf16[128,8,128]{2,1,0:T(8,128)(2,1)}, u32[]{:S(2)}) copy-start(bf16[128,8,128]{2,1,0:T(8,128)(2,1)} %param.21) | copy-start | bytes 786436
  0.7 19.3 %copy-start.6 = (s32[128]{0:T(128)S(1)}, s32[128]{0:T(128)}, u32[]{:S(2)}) copy-start(s32[128]{0:T(128)} %param.22) | copy-start | bytes 1540
  0.7 24.4 %copy-start.2 = (s32[128,8]{0,1:T(8,128)S(1)}, s32[128,8]{0,1:T(8,128)}, u32[]{:S(2)}) copy-start(s32[128,8]{0,1:T(8,128)} %param.20) | copy-start | bytes 12292
  0.7 24.4 %copy-start.3 = (s32[128,8]{0,1:T(8,128)S(1)}, s32[128,8]{0,1:T(8,128)}, u32[]{:S(2)}) copy-start(s32[128,8]{0,1:T(8,128)} %param.23) | copy-start | bytes 12292
  0.7 26.5 %copy-start.4 = (f32[128,8]{0,1:T(8,128)S(1)}, f32[128,8]{0,1:T(8,128)}, u32[]{:S(2)}) copy-start(f32[128,8]{0,1:T(8,128)} %param.24) | copy-start | bytes 12292
  0.7 27.3 %copy-start.5 = (f32[8,128]{1,0:T(8,128)S(1)}, f32[8,128]{1,0:T(8,128)}, u32[]{:S(2)}) copy-start(f32[8,128]{1,0:T(8,128)} %param.25) | copy-start | bytes 12292
  4.0 138.4 %all-to-all-start = ((bf16[64,8,8,128]{3,2,1,0:T(8,128)(2,1)}), bf16[64,8,8,128]{3,2,1,0:T(8,128)(2,1)S(1)}, u32[]{:S(2)}, u32[]{:S(2)}) async-start(bf16[64,8,8,128]{3,2,1,0:T(8,128)(2,1)} %bitcast.2), calls=%async_computation | async-start | bytes 2097152 | tf_op jit(solution)/shard_map/all_to_all | solution.py:21
where the time goes:
time: 363 us; the launch traced here: 361 us
  blocking collectives  247 us (68%)
  local copies, waits for them, and re-layouts  64.4 us (18%)
  matrix products  26.6 us (7%)
  starting transfers between devices  14.8 us (4%)
  other arithmetic  7.73 us (2%)
    all_gather x3, blocking collectives, shards(): arrived_colour = lax.all_gather(fresh, 'tile', axis=1, tiled=True)  128 us
    all_gather x1, blocking collectives, shards(): lax.all_gather(start_group, 'tile', axis=2, tiled=True)  54.6 us
    all_gather x1, blocking collectives, shards(): lax.all_gather(own_flat, 'tile', axis=0, tiled=True)  49.7 us
    transpose x4, local copies, waits for them, and re-layouts, project(): jnp.einsum('kjs,kjv->svk', one_hot, weight_rows, preferred_element_type=j...  32.1 us
    all_to_all x1, starting transfers between devices, shards(): lax.all_to_all(outgoing, 'tile', split_axis=0, concat_axis=0, tiled=True)  14.8 us
    psum x1, blocking collectives, shards(): energy_sum = lax.psum(jnp.sum(traces * traces, axis=0), 'tm')  13.9 us
    dot_general x4, matrix products, project(): jnp.einsum('sfv,svk->fk', arrived, spread, preferred_element_type=jnp.flo...  13.5 us
    dot_general x4, matrix products, project(): jnp.einsum('kjs,kjv->svk', one_hot, weight_rows, preferred_element_type=j...  13.1 us
  transfers between devices with their start and end apart: 1, of which 0 were waited for; matrix products, arithmetic and copies ran while one was open for 5% of the time, Pallas kernels for 0%

commit v1 on v0

v1 whole, which is shorter than its diff:
```python
import functools

import jax
import jax.numpy as jnp
from jax import lax
from jax.experimental import pallas as pl
from jax.experimental.pallas import tpu as pltpu
from jax.sharding import PartitionSpec as P

MESH = pl.DeviceIdType.MESH
COLOURS = 4
STRIDE = 27


def sweep_kernel(
    tiles, groups, data, send, slots, footprint, colour, correlation, gram, init,
    traces_out, rms_out, outgoing, arrived, table, mine, parts,
    block_send, block_recv, near_send, near_recv, part_send, part_recv,
):
    me = lax.axis_index("tile")
    row = lax.axis_index("tm")
    cap = send.shape[0]
    blocks_fp, comps = slots.shape
    frames_dev, voxels = data.shape[1:]
    listed = correlation.shape[0]
    left = lax.rem(me + tiles - 1, tiles)
    right = lax.rem(me + 1, tiles)
    far = lax.rem(me + tiles // 2, tiles)

    barrier = pltpu.get_barrier_semaphore()

    def greet_tile(step, carry):
        peer = lax.rem(me + step * STRIDE, tiles)
        pl.semaphore_signal(barrier, inc=1, device_id={"tile": peer}, device_id_type=MESH)
        return carry

    def greet_row(step, carry):
        peer = lax.rem(row + step, groups)
        pl.semaphore_signal(barrier, inc=1, device_id={"tm": peer}, device_id_type=MESH)
        return carry

    lax.fori_loop(1, tiles, greet_tile, 0)
    lax.fori_loop(1, groups, greet_row, 0)

    def collect(owner, carry):
        for slot in range(cap):
            outgoing[owner * cap + slot] = data[send[slot, owner]]
        return carry

    lax.fori_loop(0, tiles, collect, 0)
    for slot in range(cap):
        arrived[me * cap + slot] = outgoing[me * cap + slot]

    pl.semaphore_wait(barrier, tiles - 1 + groups - 1)

    def near_copies(source, version):
        return [
            pltpu.make_async_remote_copy(
                src_ref=source,
                dst_ref=table.at[version, region],
                send_sem=near_send.at[version, region],
                recv_sem=near_recv.at[version, region],
                device_id={"tile": peer},
                device_id_type=MESH,
            )
            for region, peer in ((2, far), (0, right), (1, left))
        ]

    def block_copy(step):
        peer = lax.rem(me + step * STRIDE, tiles)
        return pltpu.make_async_remote_copy(
            src_ref=outgoing.at[pl.ds(peer * cap, cap)],
            dst_ref=arrived.at[pl.ds(me * cap, cap)],
            send_sem=block_send.at[peer],
            recv_sem=block_recv.at[me],
            device_id={"tile": peer},
            device_id_type=MESH,
        )

    def block_start(step, carry):
        block_copy(step).start()
        return carry

    lax.fori_loop(1, tiles, block_start, 0)
    copies = near_copies(init, 0)
    for copy in copies:
        copy.start()

    lane = lax.broadcasted_iota(jnp.int32, (frames_dev, comps), 1)
    zero = jnp.zeros((frames_dev, comps), jnp.float32)
    unroll = 8

    def square(step, total):
        for inner in range(unroll):
            comp = step * unroll + inner
            weights = footprint[comp].astype(jnp.float32)
            column = jnp.sum(weights * weights, axis=1, keepdims=True)
            total = jnp.where(lane == comp, column, total)
        return total

    squares = lax.fori_loop(0, comps // unroll, square, zero)
    self_gram = jnp.broadcast_to(jnp.sum(squares, axis=0, keepdims=True), zero.shape)
    ids = correlation[...]
    owner = lax.shift_right_logical(ids, comps.bit_length() - 1)
    local = ids & (comps - 1)
    code = jnp.where(owner == left, 0, jnp.where(owner == right, 1, jnp.where(owner == far, 2, 3)))
    coupling = gram[...]

    def spread(values, entry):
        return jnp.broadcast_to(values[entry : entry + 1, :], zero.shape)

    codes = [spread(code, entry) for entry in range(listed)]
    locals_ = [spread(local, entry) for entry in range(listed)]
    couplings = [spread(coupling, entry) for entry in range(listed)]
    shade = jnp.broadcast_to(colour[...], zero.shape)

    def block_wait(step, carry):
        source = lax.rem(me + tiles * STRIDE - step * STRIDE, tiles)
        pltpu.make_async_remote_copy(
            src_ref=outgoing.at[pl.ds(source * cap, cap)],
            dst_ref=arrived.at[pl.ds(source * cap, cap)],
            send_sem=block_send.at[source],
            recv_sem=block_recv.at[source],
            device_id={"tile": source},
            device_id_type=MESH,
        ).wait()
        return carry

    lax.fori_loop(1, tiles, block_wait, 0)

    def project(step, total):
        for inner in range(unroll):
            comp = step * unroll + inner
            weights = footprint[comp].astype(jnp.float32)
            products = jnp.zeros((frames_dev, voxels), jnp.float32)
            for entry in range(blocks_fp):
                block = arrived[slots[entry, comp]].astype(jnp.float32)
                products = products + block * weights[entry : entry + 1, :]
            column = jnp.sum(products, axis=1, keepdims=True)
            total = jnp.where(lane == comp, column, total)
        return total

    projected = lax.fori_loop(0, comps // unroll, project, zero)

    current = init[...]
    for step_colour in range(COLOURS):
        for copy in copies:
            copy.wait()
        sides = [table[step_colour, region] for region in range(3)]
        neighbour_sum = zero
        for entry in range(listed):
            index = locals_[entry]
            picked = jnp.take_along_axis(current, index, axis=1)
            for region in range(3):
                side = jnp.take_along_axis(sides[region], index, axis=1)
                picked = jnp.where(codes[entry] == region, side, picked)
            neighbour_sum = neighbour_sum + couplings[entry] * picked
        fresh = jnp.maximum((projected - neighbour_sum) / self_gram, 0.0)
        current = jnp.where(shade == step_colour, fresh, current)
        if step_colour + 1 < COLOURS:
            mine[step_colour] = current
            copies = near_copies(mine.at[step_colour], step_colour + 1)
            for copy in copies:
                copy.start()
    traces_out[...] = current

    parts[row] = jnp.sum(current * current, axis=0, keepdims=True)

    def part_start(step, carry):
        peer = lax.rem(row + step, groups)
        pltpu.make_async_remote_copy(
            src_ref=parts.at[row],
            dst_ref=parts.at[row],
            send_sem=part_send.at[peer],
            recv_sem=part_recv.at[row],
            device_id={"tm": peer},
            device_id_type=MESH,
        ).start()
        return carry

    def part_wait(step, carry):
        source = lax.rem(row + step, groups)
        pltpu.make_async_remote_copy(
            src_ref=parts.at[source],
            dst_ref=parts.at[source],
            send_sem=part_send.at[source],
            recv_sem=part_recv.at[source],
            device_id={"tm": source},
            device_id_type=MESH,
        ).wait()
        return carry

    lax.fori_loop(1, groups, part_start, 0)
    lax.fori_loop(1, groups, part_wait, 0)
    energy = parts[0]
    for group in range(1, groups):
        energy = energy + parts[group]
    rms_out[...] = jnp.sqrt(energy / (frames_dev * groups) + 1e-06)


def shards(
    tiles, groups, data, send_list, footprint_slot, footprint, colour, correlation, correlation_gram, traces_init
):
    comps = colour.shape[0]
    frames_dev, voxels = data.shape[1:]
    cap = send_list.shape[2]
    vmem = pl.BlockSpec(memory_space=pltpu.VMEM)
    smem = pl.BlockSpec(memory_space=pltpu.SMEM)
    traces, trace_rms = pl.pallas_call(
        functools.partial(sweep_kernel, tiles, groups),
        out_shape=(
            jax.ShapeDtypeStruct((frames_dev, comps), jnp.float32),
            jax.ShapeDtypeStruct((1, comps), jnp.float32),
        ),
        in_specs=[vmem, smem, smem, vmem, vmem, vmem, vmem, vmem],
        out_specs=(vmem, vmem),
        scratch_shapes=[
            pltpu.VMEM((tiles * cap, frames_dev, voxels), data.dtype),
            pltpu.VMEM((tiles * cap, frames_dev, voxels), data.dtype),
            pltpu.VMEM((COLOURS, 3, frames_dev, comps), jnp.float32),
            pltpu.VMEM((COLOURS - 1, frames_dev, comps), jnp.float32),
            pltpu.VMEM((groups, 1, comps), jnp.float32),
            pltpu.SemaphoreType.DMA((tiles,)),
            pltpu.SemaphoreType.DMA((tiles,)),
            pltpu.SemaphoreType.DMA((COLOURS, 3)),
            pltpu.SemaphoreType.DMA((COLOURS, 3)),
            pltpu.SemaphoreType.DMA((groups,)),
            pltpu.SemaphoreType.DMA((groups,)),
        ],
        compiler_params=pltpu.CompilerParams(collective_id=0, has_side_effects=True),
        name="trace_sweep",
    )(
        data,
        send_list[0].T,
        footprint_slot.T,
        footprint,
        colour.reshape(1, comps),
        correlation.T,
        correlation_gram.T,
        traces_init,
    )
    return traces, trace_rms.reshape(comps)


def solution(mesh):
    placed = (
        P("tile", "tm", None),
        P("tile", None, None),
        P("tile", None),
        P("tile", None, None),
        P("tile"),
        P("tile", None),
        P("tile", None),
        P("tm", "tile"),
    )
    return jax.shard_map(
        functools.partial(shards, mesh.shape["tile"], mesh.shape["tm"]),
        mesh=mesh,
        in_specs=placed,
        out_specs=(P("tm", "tile"), P("tile")),
        check_vma=False,
    )
```

time: 363 us -> 69.7 us (0.19)
  the two profiles are of different devices: /device:TPU:1 before, /device:TPU:8 now
where the time goes in v1:
time: 69.7 us; the launch traced here: 69.5 us
  Pallas kernels  67 us (96%)
  local copies, waits for them, and re-layouts  1.82 us (3%)
    pallas_call x1, Pallas kernels, shards(): pl.pallas_call(functools.partial(sweep_kernel, tiles, groups), out_shape=...  67 us
    unnamed x6, local copies, waits for them, and re-layouts  1.82 us

profile of v1, /device:TPU:8, one launch (start us, length us, event | category | flops | bytes accessed | tf_op | source)
XLA Modules:
  0.0 69.5 jit_solution(4347018209665076189)
XLA Ops:
  0.6 67.0 %trace_sweep.1 = (f32[8,128]{1,0:T(8,128)}, f32[1,128]{1,0:T(1,128)}) custom-call(bf16[128,8,128]{2,1,0:T(8,128)(2,1)} %data.1, s32[8,64]{1,0:T(8,128)} %bitcast.8, s32[8,128]{1,0:T(8,128)} %bitcast.9, bf16[128,8,128]{2,1,0:T(8,128)(2,1)} %footprint.1, s32[1,128]{1,0:T(1,128)} %bitcast.12, s32[8,128]{1,0:T(8,128)} %bitcast.10, f32[8,128]{1,0:T(8,128)} %bitcast.11, ...), custom_call_target="tpu_custom_call" | custom-call | tf_op jit(solution)/shard_map/trace_sweep/pallas_call | solution.py:209
  67.7 0.0 copy-start
  67.7 0.7 copy-done
  68.3 0.0 copy-start.1
  68.3 0.6 copy.12
  68.9 0.0 copy-done.1
  69.0 0.5 copy.13
Async XLA Ops:
  67.7 0.7 copy-start
  68.3 0.6 copy-start.1

commit v2 on v1

v2 whole, which is shorter than its diff:
```python
import functools

import jax
import jax.numpy as jnp
from jax import lax
from jax.experimental import pallas as pl
from jax.experimental.pallas import tpu as pltpu
from jax.sharding import PartitionSpec as P

MESH = pl.DeviceIdType.MESH
INNER = 8


def offsets_within(tiles):
    half = tiles // 2
    reach = {0}
    rings = []
    for _ in range(3):
        reach = {(at + move) % tiles for at in reach for move in (0, 1, -1, half)}
        rings.append(reach)
    first, second, third = rings
    close = sorted(second - {0})
    return sorted(first), close, close + sorted(third - second)


def sweep_kernel(
    tiles, groups, data, send, slots, footprint, colour, correlation, gram, init,
    traces_out, energy_out, outgoing, arrived, near_init, near_ids, near_gram, near_rows,
    rows, mixed, near_mixed, parts,
    block_send, block_recv, near_send, near_recv, mixed_send, mixed_recv, part_send, part_recv,
):
    me = lax.axis_index("tile")
    row = lax.axis_index("tm")
    cap = send.shape[0]
    blocks_fp, comps = slots.shape
    frames_dev, voxels = data.shape[1:]
    listed = correlation.shape[0]
    half = tiles // 2
    inner_count = min(INNER, tiles)
    outer_count = tiles // inner_count
    outer_half = outer_count // 2
    outer = me // inner_count
    inner = lax.rem(me, inner_count)
    adjacent, close, reached = offsets_within(tiles)

    barrier = pltpu.get_barrier_semaphore()

    def greet_tile(step, carry):
        peer = lax.rem(me + step, tiles)
        pl.semaphore_signal(barrier, inc=1, device_id={"tile": peer}, device_id_type=MESH)
        return carry

    def greet_row(step, carry):
        peer = lax.rem(row + step, groups)
        pl.semaphore_signal(barrier, inc=1, device_id={"tm": peer}, device_id_type=MESH)
        return carry

    lax.fori_loop(1, tiles, greet_tile, 0)
    lax.fori_loop(1, groups, greet_row, 0)

    def collect(owner, carry):
        for slot in range(cap):
            outgoing[owner * cap + slot] = data[send[slot, owner]]
        return carry

    lax.fori_loop(0, tiles, collect, 0)
    for slot in range(cap):
        arrived[me * cap + slot] = outgoing[me * cap + slot]

    pl.semaphore_wait(barrier, tiles - 1 + groups - 1)

    def block_start(outer_step, inner_step):
        peer = lax.rem(outer + outer_step, outer_count) * inner_count + lax.rem(inner + inner_step, inner_count)
        pltpu.make_async_remote_copy(
            src_ref=outgoing.at[pl.ds(peer * cap, cap)],
            dst_ref=arrived.at[pl.ds(me * cap, cap)],
            send_sem=block_send.at[peer],
            recv_sem=block_recv.at[me],
            device_id={"tile": peer},
            device_id_type=MESH,
        ).start()

    def opposite_start(step, carry):
        block_start(outer_half, step)
        return carry

    def paired_start(step, carry):
        distance = outer_half - 1 - step // (2 * inner_count)
        within = lax.rem(step, 2 * inner_count)
        way = lax.rem(within, 2)
        block_start(distance + way * (outer_count - 2 * distance), within // 2)
        return carry

    def local_start(step, carry):
        block_start(0, step)
        return carry

    if outer_count > 1:
        lax.fori_loop(0, inner_count, opposite_start, 0)
        lax.fori_loop(0, (outer_half - 1) * 2 * inner_count, paired_start, 0)
    lax.fori_loop(1, inner_count, local_start, 0)

    lane = lax.broadcasted_iota(jnp.int32, (frames_dev, comps), 1)
    zero = jnp.zeros((frames_dev, comps), jnp.float32)
    unroll = 8

    def square(step, total):
        for within in range(unroll):
            comp = step * unroll + within
            weights = footprint[comp].astype(jnp.float32)
            column = jnp.sum(weights * weights, axis=1, keepdims=True)
            total = jnp.where(lane == comp, column, total)
        return total

    squares = lax.fori_loop(0, comps // unroll, square, zero)
    rows[0:1, :] = jnp.sum(squares, axis=0, keepdims=True)
    rows[1:2, :] = colour[...].astype(jnp.float32)

    def near_copies(offset):
        peer = lax.rem(me + offset, tiles)
        place = close.index((tiles - offset) % tiles)
        return [
            pltpu.make_async_remote_copy(
                src_ref=source,
                dst_ref=target.at[place],
                send_sem=near_send.at[kind, place],
                recv_sem=near_recv.at[kind, place],
                device_id={"tile": peer},
                device_id_type=MESH,
            )
            for kind, (source, target) in enumerate(
                ((init, near_init), (correlation, near_ids), (gram, near_gram), (rows, near_rows))
            )
        ]

    statics = {offset: near_copies(offset) for offset in close}
    for kind in range(4):
        for offset in close:
            statics[offset][kind].start()

    def block_wait(step, carry):
        source = lax.rem(me + step, tiles)
        pltpu.make_async_remote_copy(
            src_ref=outgoing.at[pl.ds(source * cap, cap)],
            dst_ref=arrived.at[pl.ds(source * cap, cap)],
            send_sem=block_send.at[source],
            recv_sem=block_recv.at[source],
            device_id={"tile": source},
            device_id_type=MESH,
        ).wait()
        return carry

    lax.fori_loop(1, tiles, block_wait, 0)

    def project(step, total):
        for within in range(unroll):
            comp = step * unroll + within
            weights = footprint[comp].astype(jnp.float32)
            products = jnp.zeros((frames_dev, voxels), jnp.float32)
            for entry in range(blocks_fp):
                block = arrived[slots[entry, comp]].astype(jnp.float32)
                products = products + block * weights[entry : entry + 1, :]
            column = jnp.sum(products, axis=1, keepdims=True)
            total = jnp.where(lane == comp, column, total)
        return total

    projected = lax.fori_loop(0, comps // unroll, project, zero)

    def update(offset, step_colour, values, sums, ids, weights, energy, shade):
        around = [values[(offset + move) % tiles] for move in (1, tiles - 1, half, 0)]
        owner = lax.shift_right_logical(ids, comps.bit_length() - 1)
        local = ids & (comps - 1)
        code = jnp.where(owner == lax.rem(me + offset + half, tiles), 2, 3)
        code = jnp.where(owner == lax.rem(me + offset + tiles - 1, tiles), 1, code)
        code = jnp.where(owner == lax.rem(me + offset + 1, tiles), 0, code)
        neighbour_sum = zero
        for entry in range(listed):
            index = jnp.broadcast_to(local[entry : entry + 1, :], zero.shape)
            which = jnp.broadcast_to(code[entry : entry + 1, :], zero.shape)
            weight = jnp.broadcast_to(weights[entry : entry + 1, :], zero.shape)
            picked = jnp.take_along_axis(around[3], index, axis=1)
            for region in range(3):
                side = jnp.take_along_axis(around[region], index, axis=1)
                picked = jnp.where(which == region, side, picked)
            neighbour_sum = neighbour_sum + weight * picked
        fresh = jnp.maximum((sums - neighbour_sum) / energy, 0.0)
        return jnp.where(shade == step_colour, fresh, values[offset])

    def waited(offset, kind):
        copy = statics[(tiles - offset) % tiles][kind]
        copy.wait()

    facts = {0: (correlation[...], gram[...], rows[0:1, :], rows[1:2, :].astype(jnp.int32))}
    for offset in close:
        waited(offset, 0)
    starts = {offset: near_init[place] for place, offset in enumerate(close)}
    starts[0] = init[...]
    values = {0: update(0, 0, starts, projected, *facts[0])}
    mixed[0] = jnp.where(facts[0][3] == 0, values[0], projected)
    mixed[1] = values[0]
    mixes = []
    for offset in reversed(reached):
        place = reached.index((tiles - offset) % tiles)
        mixes.append(
            pltpu.make_async_remote_copy(
                src_ref=mixed.at[0 if offset in close else 1],
                dst_ref=near_mixed.at[place],
                send_sem=mixed_send.at[place],
                recv_sem=mixed_recv.at[place],
                device_id={"tile": lax.rem(me + offset, tiles)},
                device_id_type=MESH,
            )
        )
    for copy in mixes:
        copy.start()
    for offset in close:
        for kind in range(1, 4):
            waited(offset, kind)
    for place, offset in enumerate(close):
        facts[offset] = (
            near_ids[place],
            near_gram[place],
            near_rows[place, 0:1, :],
            near_rows[place, 1:2, :].astype(jnp.int32),
        )
    for copy in mixes:
        copy.wait()

    sums = {0: projected}
    for place, offset in enumerate(reached):
        values[offset] = near_mixed[place]
    for offset in close:
        sums[offset] = values[offset]
        values[offset] = jnp.where(facts[offset][3] == 0, sums[offset], starts[offset])
    for step_colour, area in ((1, [0] + close), (2, adjacent), (3, [0])):
        renewed = {offset: update(offset, step_colour, values, sums[offset], *facts[offset]) for offset in area}
        values = renewed
    current = values[0]
    traces_out[...] = current

    parts[row] = jnp.sum(current * current, axis=0, keepdims=True)

    def part_start(step, carry):
        peer = lax.rem(row + step, groups)
        pltpu.make_async_remote_copy(
            src_ref=parts.at[row],
            dst_ref=parts.at[row],
            send_sem=part_send.at[peer],
            recv_sem=part_recv.at[row],
            device_id={"tm": peer},
            device_id_type=MESH,
        ).start()
        return carry

    def part_wait(step, carry):
        source = lax.rem(row + step, groups)
        pltpu.make_async_remote_copy(
            src_ref=parts.at[source],
            dst_ref=parts.at[source],
            send_sem=part_send.at[source],
            recv_sem=part_recv.at[source],
            device_id={"tm": source},
            device_id_type=MESH,
        ).wait()
        return carry

    lax.fori_loop(1, groups, part_start, 0)
    lax.fori_loop(1, groups, part_wait, 0)
    energy = parts[0]
    for group in range(1, groups):
        energy = energy + parts[group]
    energy_out[...] = energy


def shards(
    tiles, groups, data, send_list, footprint_slot, footprint, colour, correlation, correlation_gram, traces_init
):
    comps = colour.shape[0]
    frames_dev, voxels = data.shape[1:]
    cap = send_list.shape[2]
    vmem = pl.BlockSpec(memory_space=pltpu.VMEM)
    smem = pl.BlockSpec(memory_space=pltpu.SMEM)
    _, close, reached = offsets_within(tiles)
    tile_shape = (frames_dev, comps)
    list_shape = (correlation.shape[1], comps)
    traces, energy = pl.pallas_call(
        functools.partial(sweep_kernel, tiles, groups),
        out_shape=(
            jax.ShapeDtypeStruct((frames_dev, comps), jnp.float32),
            jax.ShapeDtypeStruct((1, comps), jnp.float32),
        ),
        in_specs=[vmem, smem, smem, vmem, vmem, vmem, vmem, vmem],
        out_specs=(vmem, vmem),
        scratch_shapes=[
            pltpu.VMEM((tiles * cap, frames_dev, voxels), data.dtype),
            pltpu.VMEM((tiles * cap, frames_dev, voxels), data.dtype),
            pltpu.VMEM((len(close),) + tile_shape, jnp.float32),
            pltpu.VMEM((len(close),) + list_shape, jnp.int32),
            pltpu.VMEM((len(close),) + list_shape, jnp.float32),
            pltpu.VMEM((len(close), 2, comps), jnp.float32),
            pltpu.VMEM((2, comps), jnp.float32),
            pltpu.VMEM((2,) + tile_shape, jnp.float32),
            pltpu.VMEM((len(reached),) + tile_shape, jnp.float32),
            pltpu.VMEM((groups, 1, comps), jnp.float32),
            pltpu.SemaphoreType.DMA((tiles,)),
            pltpu.SemaphoreType.DMA((tiles,)),
            pltpu.SemaphoreType.DMA((4, len(close))),
            pltpu.SemaphoreType.DMA((4, len(close))),
            pltpu.SemaphoreType.DMA((len(reached),)),
            pltpu.SemaphoreType.DMA((len(reached),)),
            pltpu.SemaphoreType.DMA((groups,)),
            pltpu.SemaphoreType.DMA((groups,)),
        ],
        compiler_params=pltpu.CompilerParams(collective_id=0, has_side_effects=True),
        name="trace_sweep",
    )(
        data,
        send_list[0].T,
        footprint_slot.T,
        footprint,
        colour.reshape(1, comps),
        correlation.T,
        correlation_gram.T,
        traces_init,
    )
    trace_rms = jnp.sqrt(energy.reshape(comps) / (frames_dev * groups) + 1e-06)
    return jnp.maximum(traces, 0.0), trace_rms


def solution(mesh):
    placed = (
        P("tile", "tm", None),
        P("tile", None, None),
        P("tile", None),
        P("tile", None, None),
        P("tile"),
        P("tile", None),
        P("tile", None),
        P("tm", "tile"),
    )
    return jax.shard_map(
        functools.partial(shards, mesh.shape["tile"], mesh.shape["tm"]),
        mesh=mesh,
        in_specs=placed,
        out_specs=(P("tm", "tile"), P("tile")),
        check_vma=False,
    )
```

time: 69.7 us -> 62.1 us (0.89)
  the two profiles are of different devices: /device:TPU:8 before, /device:TPU:1 now
where the time goes in v2:
time: 62.1 us; the launch traced here: 62 us
  Pallas kernels  59.5 us (96%)
  other arithmetic  1.79 us (3%)
  between operations  0.65 us (1%)
    pallas_call x1, Pallas kernels, shards(): pl.pallas_call(functools.partial(sweep_kernel, tiles, groups), out_shape=...  59.5 us
    max x1, other arithmetic, shards(): return (jnp.maximum(traces, 0.0), trace_rms)  1.27 us

profile of v2, /device:TPU:1, one launch (start us, length us, event | category | flops | bytes accessed | tf_op | source)
XLA Modules:
  0.0 62.0 jit_solution(9331200796861992872)
XLA Ops:
  0.6 59.5 %trace_sweep.1 = (f32[8,128]{1,0:T(8,128)}, f32[1,128]{1,0:T(1,128)}) custom-call(bf16[128,8,128]{2,1,0:T(8,128)(2,1)} %data.1, s32[8,64]{1,0:T(8,128)} %bitcast.9, s32[8,128]{1,0:T(8,128)} %bitcast.10, bf16[128,8,128]{2,1,0:T(8,128)(2,1)} %footprint.1, s32[1,128]{1,0:T(1,128)} %bitcast.13, s32[8,128]{1,0:T(8,128)} %bitcast.11, f32[8,128]{1,0:T(8,128)} %bitcast.12, ...), custom_call_target="tpu_custom_call" | custom-call | tf_op jit(solution)/shard_map/trace_sweep/pallas_call | solution.py:286
  60.2 0.0 copy-start
  60.2 1.3 %broadcast_maximum_fusion = f32[8,128]{1,0:T(8,128)} fusion(f32[8,128]{1,0:T(8,128)} %get-tuple-element.4), kind=kLoop, calls=%fused_computation | loop fusion | flops 1024 | bytes 8192 | tf_op jit(solution)/shard_map/max | solution.py:327
  61.4 0.0 copy-done
  61.4 0.5 sqrt_bitcast_fusion
Async XLA Ops:
  60.2 1.3 %copy-start = (f32[1,128]{1,0:T(1,128)S(1)}, f32[1,128]{1,0:T(1,128)}, u32[]{:S(2)}) copy-start(f32[1,128]{1,0:T(1,128)} %get-tuple-element.5) | copy-start | bytes 1540

commit v3 on v2

--- a/solution.py
+++ b/solution.py
@@ -24,8 +24,9 @@
 
 
 def sweep_kernel(
-    tiles, groups, data, send, slots, footprint, colour, correlation, gram, init,
-    traces_out, energy_out, outgoing, arrived, near_init, near_ids, near_gram, near_rows,
+    tiles, groups, data_in, send_in, slots_in, footprint_in, colour_in, correlation_in, gram_in, init_in,
+    traces_out, energy_out, data, send, slots, footprint, colour, correlation, gram, init, load_sem,
+    wide_blocks, wide_weights, outgoing, arrived, near_init, near_ids, near_gram, near_rows,
     rows, mixed, near_mixed, parts,
     block_send, block_recv, near_send, near_recv, mixed_send, mixed_recv, part_send, part_recv,
 ):
@@ -58,6 +59,20 @@
     lax.fori_loop(1, tiles, greet_tile, 0)
     lax.fori_loop(1, groups, greet_row, 0)
 
+    loads = [
+        pltpu.make_async_copy(source, target, load_sem.at[place])
+        for place, (source, target) in enumerate(
+            (
+                (data_in, data), (send_in, send), (footprint_in, footprint), (init_in, init),
+                (colour_in, colour), (correlation_in, correlation), (gram_in, gram), (slots_in, slots),
+            )
+        )
+    ]
+    for load in loads:
+        load.start()
+    for load in loads[:2]:
+        load.wait()
+
     def collect(owner, carry):
         for slot in range(cap):
             outgoing[owner * cap + slot] = data[send[slot, owner]]
@@ -65,12 +80,38 @@
 
     lax.fori_loop(0, tiles, collect, 0)
     for slot in range(cap):
-        arrived[me * cap + slot] = outgoing[me * cap + slot]
+        wide_blocks[me * cap + slot] = outgoing[me * cap + slot].astype(jnp.float32)
+    for load in loads[2:]:
+        load.wait()
 
     pl.semaphore_wait(barrier, tiles - 1 + groups - 1)
 
+    def tile_at(outer_step, inner_step):
+        return lax.rem(outer + outer_step, outer_count) * inner_count + lax.rem(inner + inner_step, inner_count)
+
+    def every_pair(act):
+        def opposite(step, carry):
+            act(outer_half, step)
+            return carry
+
+        def paired(step, carry):
+            distance = outer_half - 1 - step // (2 * inner_count)
+            within = lax.rem(step, 2 * inner_count)
+            way = lax.rem(within, 2)
+            act(distance + way * (outer_count - 2 * distance), within // 2)
+            return carry
+
+        def local(step, carry):
+            act(0, step)
+            return carry
+
+        if outer_count > 1:
+            lax.fori_loop(0, inner_count, opposite, 0)
+            lax.fori_loop(0, (outer_half - 1) * 2 * inner_count, paired, 0)
+        lax.fori_loop(1, inner_count, local, 0)
+
     def block_start(outer_step, inner_step):
-        peer = lax.rem(outer + outer_step, outer_count) * inner_count + lax.rem(inner + inner_step, inner_count)
+        peer = tile_at(outer_step, inner_step)
         pltpu.make_async_remote_copy(
             src_ref=outgoing.at[pl.ds(peer * cap, cap)],
             dst_ref=arrived.at[pl.ds(me * cap, cap)],
@@ -80,34 +121,17 @@
             device_id_type=MESH,
         ).start()
 
-    def opposite_start(step, carry):
-        block_start(outer_half, step)
-        return carry
-
-    def paired_start(step, carry):
-        distance = outer_half - 1 - step // (2 * inner_count)
-        within = lax.rem(step, 2 * inner_count)
-        way = lax.rem(within, 2)
-        block_start(distance + way * (outer_count - 2 * distance), within // 2)
-        return carry
-
-    def local_start(step, carry):
-        block_start(0, step)
-        return carry
-
-    if outer_count > 1:
-        lax.fori_loop(0, inner_count, opposite_start, 0)
-        lax.fori_loop(0, (outer_half - 1) * 2 * inner_count, paired_start, 0)
-    lax.fori_loop(1, inner_count, local_start, 0)
+    every_pair(block_start)
 
     lane = lax.broadcasted_iota(jnp.int32, (frames_dev, comps), 1)
     zero = jnp.zeros((frames_dev, comps), jnp.float32)
-    unroll = 8
+    unroll = 16
 
     def square(step, total):
         for within in range(unroll):
             comp = step * unroll + within
             weights = footprint[comp].astype(jnp.float32)
+            wide_weights[pl.ds(pl.multiple_of(comp * blocks_fp, blocks_fp), blocks_fp), :] = weights
             column = jnp.sum(weights * weights, axis=1, keepdims=True)
             total = jnp.where(lane == comp, column, total)
         return total
@@ -138,8 +162,8 @@
         for offset in close:
             statics[offset][kind].start()
 
-    def block_wait(step, carry):
-        source = lax.rem(me + step, tiles)
+    def block_wait(outer_step, inner_step):
+        source = tile_at(outer_step, inner_step)
         pltpu.make_async_remote_copy(
             src_ref=outgoing.at[pl.ds(source * cap, cap)],
             dst_ref=arrived.at[pl.ds(source * cap, cap)],
@@ -148,18 +172,18 @@
             device_id={"tile": source},
             device_id_type=MESH,
         ).wait()
-        return carry
-
-    lax.fori_loop(1, tiles, block_wait, 0)
+        for slot in range(cap):
+            wide_blocks[source * cap + slot] = arrived[source * cap + slot].astype(jnp.float32)
+
+    every_pair(block_wait)
 
     def project(step, total):
         for within in range(unroll):
             comp = step * unroll + within
-            weights = footprint[comp].astype(jnp.float32)
             products = jnp.zeros((frames_dev, voxels), jnp.float32)
             for entry in range(blocks_fp):
-                block = arrived[slots[entry, comp]].astype(jnp.float32)
-                products = products + block * weights[entry : entry + 1, :]
+                weights = wide_weights[pl.ds(comp * blocks_fp + entry, 1), :]
+                products = products + wide_blocks[slots[entry, comp]] * weights
             column = jnp.sum(products, axis=1, keepdims=True)
             total = jnp.where(lane == comp, column, total)
         return total
@@ -279,7 +303,8 @@
     frames_dev, voxels = data.shape[1:]
     cap = send_list.shape[2]
     vmem = pl.BlockSpec(memory_space=pltpu.VMEM)
-    smem = pl.BlockSpec(memory_space=pltpu.SMEM)
+    anywhere = pl.BlockSpec(memory_space=pl.ANY)
+    slot_total, blocks_fp = tiles * cap, footprint.shape[1]
     _, close, reached = offsets_within(tiles)
     tile_shape = (frames_dev, comps)
     list_shape = (correlation.shape[1], comps)
@@ -289,9 +314,20 @@
             jax.ShapeDtypeStruct((frames_dev, comps), jnp.float32),
             jax.ShapeDtypeStruct((1, comps), jnp.float32),
         ),
-        in_specs=[vmem, smem, smem, vmem, vmem, vmem, vmem, vmem],
+        in_specs=[anywhere] * 8,
         out_specs=(vmem, vmem),
         scratch_shapes=[
+            pltpu.VMEM(data.shape, data.dtype),
+            pltpu.SMEM((cap, tiles), jnp.int32),
+            pltpu.SMEM((blocks_fp, comps), jnp.int32),
+            pltpu.VMEM(footprint.shape, footprint.dtype),
+            pltpu.VMEM((1, comps), jnp.int32),
+            pltpu.VMEM(list_shape, jnp.int32),
+            pltpu.VMEM(list_shape, jnp.float32),
+            pltpu.VMEM(tile_shape, jnp.float32),
+            pltpu.SemaphoreType.DMA((8,)),
+            pltpu.VMEM((slot_total, frames_dev, voxels), jnp.float32),
+            pltpu.VMEM((comps * blocks_fp, voxels), jnp.float32),
             pltpu.VMEM((tiles * cap, frames_dev, voxels), data.dtype),
             pltpu.VMEM((tiles * cap, frames_dev, voxels), data.dtype),
             pltpu.VMEM((len(close),) + tile_shape, jnp.float32),

time: 62.1 us -> 60.5 us (0.974)
  Pallas kernels: 59.5 us -> 57.9 us
    pallas_call x1, Pallas kernels: 59.5 us -> 57.9 us  [shards(): pl.pallas_call(functools.partial(sweep_kernel, tiles, groups), out_shape=...]
where the time goes in v3:
time: 60.5 us; the launch traced here: 60.4 us
  Pallas kernels  57.9 us (96%)
  other arithmetic  1.79 us (3%)
  between operations  0.65 us (1%)
    pallas_call x1, Pallas kernels, shards(): pl.pallas_call(functools.partial(sweep_kernel, tiles, groups), out_shape=...  57.9 us
    max x1, other arithmetic, shards(): return (jnp.maximum(traces, 0.0), trace_rms)  1.27 us

profile of v3, /device:TPU:1, one launch (start us, length us, event | category | flops | bytes accessed | tf_op | source)
XLA Modules:
  0.0 60.4 jit_solution(10378552443218972657)
XLA Ops:
  0.6 57.9 %trace_sweep.1 = (f32[8,128]{1,0:T(8,128)}, f32[1,128]{1,0:T(1,128)}) custom-call(bf16[128,8,128]{2,1,0:T(8,128)(2,1)} %data_in.1, s32[8,64]{1,0:T(8,128)} %bitcast.9, s32[8,128]{1,0:T(8,128)} %bitcast.10, bf16[128,8,128]{2,1,0:T(8,128)(2,1)} %footprint_in.1, s32[1,128]{1,0:T(1,128)} %bitcast.13, s32[8,128]{1,0:T(8,128)} %bitcast.11, f32[8,128]{1,0:T(8,128)} %bitcast.12, ...), custom_call_target="tpu_custom_call" | custom-call | tf_op jit(solution)/shard_map/trace_sweep/pallas_call | solution.py:311
  58.6 0.0 copy-start
  58.6 1.3 %broadcast_maximum_fusion = f32[8,128]{1,0:T(8,128)} fusion(f32[8,128]{1,0:T(8,128)} %get-tuple-element.4), kind=kLoop, calls=%fused_computation | loop fusion | flops 1024 | bytes 8192 | tf_op jit(solution)/shard_map/max | solution.py:363
  59.8 0.0 copy-done
  59.8 0.5 sqrt_bitcast_fusion
Async XLA Ops:
  58.6 1.3 %copy-start = (f32[1,128]{1,0:T(1,128)S(1)}, f32[1,128]{1,0:T(1,128)}, u32[]{:S(2)}) copy-start(f32[1,128]{1,0:T(1,128)} %get-tuple-element.5) | copy-start | bytes 1540
